TPU v7x, 32 devices: a whole 2x2x4 slice. The times are simulated.
32 devices in a mesh: groups: 2 (over x), lines: 16 (over z, y, core).
Axes of the slice: x: 2, y: 2, z: 4, core: 2. Of those that a mesh axis runs over, the one named last changes fastest.
Arguments:
- raw_echo: bfloat16 [8, 2, 2048, 512], P('groups', None, 'lines'), parts along dimension 0, may hold values from -6 to 6
- range_filter: bfloat16 [2, 512, 512], replicated, may hold values from -0.1875 to 0.1875
- azimuth_phase: float32 [512, 2048], P('lines'), may hold values from -3.140625 to 3.140625
- pair_offset: int32 [4], replicated, may hold values from 1 to 3
Outputs:
- filtered: float32 [8, 2, 128, 1024], P('groups', None, None, 'lines'), parts along dimension 0
There are 2 independent parts, one for each index of `groups`. A program takes and returns all parts, laid end to end along the dimension named above; an argument that names none is the same for every part. Nothing has to cross between parts.
Inputs may be any that keep to these rules, and one draw needn't show every extreme that they name: Date d is paired with date (d + pair_offset[d]) mod 4.
All inputs are finite; a program needn't handle non-finite values.
Results may differ from a plain program's by a relative error of at most 0.0095.
Values may be sent and summed in bfloat16 or wider, within the bound.
A program may use at most 192 MiB of HBM per device.

v0:
```python
import functools

import jax
import jax.numpy as jnp
import ml_dtypes
import numpy as np
from jax import lax
from jax.experimental import pallas as pl
from jax.experimental.pallas import tpu as pltpu
from jax.sharding import PartitionSpec as P

ML_RG = 4
ML_AZ = 2
PATCH = 32
HALF = PATCH // 2
BOX_FLOOR = 0.25
LANES = 128
VMEM = pl.BlockSpec(memory_space=pltpu.VMEM)


def split_table(table):
    high = table.astype(np.float32).astype(ml_dtypes.bfloat16)
    low = (table - high.astype(np.float64)).astype(np.float32).astype(ml_dtypes.bfloat16)
    return np.stack([high, low])


def right_block(table):
    return np.block([[table.real, table.imag], [-table.imag, table.real]])


def left_block(table):
    return np.block([[table.real, -table.imag], [table.imag, table.real]])


def split(value):
    high = value.astype(jnp.bfloat16)
    low = (value - high.astype(jnp.float32)).astype(jnp.bfloat16)
    return high, low


def mm(a, b):
    return jnp.dot(a, b, preferred_element_type=jnp.float32)


def times_table(value, table):
    high, low = split(value)
    return mm(high, table[0]) + mm(low, table[0]) + mm(high, table[1])


def table_times(table, value):
    high, low = split(value)
    return mm(table[0], high) + mm(table[0], low) + mm(table[1], high)


def exact_times(value, table):
    high, low = split(value)
    return mm(high, table) + mm(low, table)


def times_exact(table, value):
    high, low = split(value)
    return mm(table, high) + mm(table, low)


def fft_leading(re, im, sign):
    count = len(re)
    if count == 1:
        return re, im
    if count == 2:
        return [re[0] + re[1], re[0] - re[1]], [im[0] + im[1], im[0] - im[1]]
    er, ei = fft_leading(re[0::2], im[0::2], sign)
    odr, odi = fft_leading(re[1::2], im[1::2], sign)
    half = count // 2
    out_r, out_i = [None] * count, [None] * count
    for k in range(half):
        angle = sign * 2.0 * np.pi * k / count
        c, s = float(np.cos(angle)), float(np.sin(angle))
        if k == 0:
            tr, ti = odr[k], odi[k]
        elif 4 * k == count:
            tr, ti = (-odi[k], odr[k]) if sign > 0 else (odi[k], -odr[k])
        else:
            tr = odr[k] * c - odi[k] * s
            ti = odr[k] * s + odi[k] * c
        out_r[k], out_i[k] = er[k] + tr, ei[k] + ti
        out_r[k + half], out_i[k + half] = er[k] - tr, ei[k] - ti
    return out_r, out_i


def compress_kernel(raw_ref, filt_ref, out_ref):
    shards = out_ref.shape[0]
    gates, line_count = filt_ref.shape[1], raw_ref.shape[2]
    weights = filt_ref[...].reshape(2 * gates, gates)
    contract = (((1,), (1,)), ((), ()))
    first = lax.dot_general(weights, raw_ref[0, 0], contract, preferred_element_type=jnp.float32)
    second = lax.dot_general(weights, raw_ref[0, 1], contract, preferred_element_type=jnp.float32)
    real = first[:gates] - second[gates:]
    imag = first[gates:] + second[:gates]
    shape = (shards, gates // shards, line_count)
    out_ref[:, 0, 0] = real.astype(jnp.bfloat16).reshape(shape)
    out_ref[:, 0, 1] = imag.astype(jnp.bfloat16).reshape(shape)


def compress(raw_echo, range_filter, shards):
    dates, _, line_count, gates = raw_echo.shape
    out = (shards, dates, 2, gates // shards, line_count)
    return pl.pallas_call(
        compress_kernel,
        grid=(dates,),
        in_specs=[
            pl.BlockSpec((1, 2, line_count, gates), lambda d: (d, 0, 0, 0)),
            pl.BlockSpec((2, gates, gates), lambda d: (0, 0, 0)),
        ],
        out_specs=pl.BlockSpec((shards, 1) + out[2:], lambda d: (0, d, 0, 0, 0)),
        out_shape=jax.ShapeDtypeStruct(out, jnp.bfloat16),
        name="compress",
    )(raw_echo, range_filter)


def focus_kernel(
    offset_ref, col_ref, cos_ref, sin_ref, twid_ref, fwd_ref, back_ref, gate_ref, main_ref, rim_ref,
    out_ref, work, focused,
):
    shards, _, _, gates, lanes = col_ref.shape
    dates = focused.shape[0]
    date = pl.program_id(0)
    chunk = min(gates, 8)
    rows = shards * gates
    for start in range(0, gates, chunk):
        part = pl.ds(start, chunk)
        re = [col_ref[s, 0, 0, part, :].astype(jnp.float32) for s in range(shards)]
        im = [col_ref[s, 0, 1, part, :].astype(jnp.float32) for s in range(shards)]
        re, im = fft_leading(re, im, -1.0)
        for k in range(shards):
            c, s = twid_ref[0, pl.ds(k, 1), :], twid_ref[1, pl.ds(k, 1), :]
            at = pl.ds(k * gates + start, chunk)
            work[at, :lanes] = re[k] * c + im[k] * s
            work[at, lanes:] = im[k] * c - re[k] * s
    spectrum = times_table(work[...], fwd_ref)
    c = cos_ref[...].reshape(rows, lanes)
    s = sin_ref[...].reshape(rows, lanes)
    re, im = spectrum[:, :lanes], spectrum[:, lanes:]
    shifted = jnp.concatenate([re * c - im * s, re * s + im * c], axis=1)
    work[...] = times_table(shifted, back_ref)
    for start in range(0, gates, chunk):
        re, im = [], []
        for k in range(shards):
            c, s = twid_ref[0, pl.ds(k, 1), :], twid_ref[1, pl.ds(k, 1), :]
            at = pl.ds(k * gates + start, chunk)
            a, b = work[at, :lanes], work[at, lanes:]
            re.append(a * c - b * s)
            im.append(b * c + a * s)
        re, im = fft_leading(re, im, 1.0)
        for n in range(shards):
            at = pl.ds(n * gates + start, chunk)
            focused[date, at, :lanes] = re[n].astype(jnp.bfloat16).astype(jnp.float32)
            focused[date, at, lanes:] = im[n].astype(jnp.bfloat16).astype(jnp.float32)

    @pl.when(date == dates - 1)
    def _():
        looks_rows = gate_ref.shape[0] // 3
        gate_looks = looks_rows // shards
        pieces = []
        rim = None
        for d in range(dates):
            partner = lax.rem(d + offset_ref[d], dates)
            a, b = focused[d, :, :lanes], focused[d, :, lanes:]
            p, q = focused[partner, :, :lanes], focused[partner, :, lanes:]
            joined = jnp.concatenate([a * p + b * q, b * p - a * q], axis=1)
            summed = times_exact(gate_ref[...], joined)
            pieces.append(exact_times(summed[:looks_rows], main_ref[...]))
            sides = jnp.concatenate([summed[looks_rows : 2 * looks_rows], summed[2 * looks_rows :]], axis=1)
            side = exact_times(sides, rim_ref[d % 2])
            if d % 2 == 0:
                rim = side
            else:
                pieces.append(rim + side)
        order = [pieces[i] for i in range(len(pieces)) if i % 3 != 2] + pieces[2::3]
        shaped = [piece.reshape(shards, gate_looks, lanes) for piece in order]
        out_ref[...] = jnp.concatenate(shaped, axis=1).astype(out_ref.dtype)


def focus_tables(shards, gates, lanes):
    total = shards * lanes
    k1, n2 = np.arange(shards), np.arange(lanes)
    angle = 2.0 * np.pi / total * (np.outer(k1, n2) % total)
    twiddle = np.stack([np.cos(angle), np.sin(angle)]).astype(np.float32)
    grid = np.exp(-2j * np.pi / lanes * (np.outer(n2, n2) % lanes))
    forward = split_table(right_block(grid))
    backward = split_table(right_block(np.conj(grid)) / total)
    group = np.kron(np.eye(gates // ML_RG), np.ones((1, ML_RG)))
    before = np.eye(shards, k=-1)
    after = np.eye(shards, k=1)
    gate_sum = np.concatenate([np.kron(m, group) for m in (np.eye(shards), before, after)])
    looks = lanes // ML_AZ
    pair = np.kron(np.eye(looks), np.ones((ML_AZ, 1))) / (ML_RG * ML_AZ)
    main = np.kron(np.eye(2), pair)
    rim = np.zeros((2, 4 * lanes, lanes))
    for parity in range(2):
        for part in range(2):
            low = parity * 4 * HALF + part * 2 * HALF
            source = part * lanes
            rim[parity, source : source + lanes, low : low + HALF] = pair[:, looks - HALF :]
            source += 2 * lanes
            rim[parity, source : source + lanes, low + HALF : low + 2 * HALF] = pair[:, :HALF]
    bf16 = ml_dtypes.bfloat16
    return twiddle, forward, backward, gate_sum.astype(bf16), main.astype(bf16), rim.astype(bf16)


def focus_looks(columns, cosine, sine, pair_offset):
    shards, dates, _, gates, lanes = columns.shape
    tables = focus_tables(shards, gates, lanes)
    rows = shards * gates
    slabs = dates + dates // 2
    whole = lambda array: pl.BlockSpec(array.shape, lambda d, *_: (0,) * array.ndim)
    out = (shards, slabs * (gates // ML_RG), lanes)
    return pl.pallas_call(
        focus_kernel,
        grid_spec=pltpu.PrefetchScalarGridSpec(
            num_scalar_prefetch=1,
            grid=(dates,),
            in_specs=[
                pl.BlockSpec((shards, 1, 2, gates, lanes), lambda d, *_: (0, d, 0, 0, 0)),
                whole(cosine),
                whole(sine),
            ]
            + [whole(table) for table in tables],
            out_specs=pl.BlockSpec(out, lambda d, *_: (0, 0, 0)),
            scratch_shapes=[
                pltpu.VMEM((rows, 2 * lanes), jnp.float32),
                pltpu.VMEM((dates, rows, 2 * lanes), jnp.float32),
            ],
        ),
        out_shape=jax.ShapeDtypeStruct(out, jnp.bfloat16),
        name="focus",
    )(pair_offset, columns, cosine, sine, *tables)


def tri_window():
    return 1.0 - np.abs(np.arange(PATCH) - (PATCH - 1) / 2.0) / HALF


def patch_maps(cells, starts):
    count = len(starts)
    forward = np.zeros((cells, count, PATCH), np.complex128)
    backward = np.zeros((count, PATCH, cells), np.complex128)
    window, k = tri_window(), np.arange(PATCH)
    for patch, start in enumerate(starts):
        for a in range(PATCH):
            cell = start + a
            if 0 <= cell < cells:
                wave = np.exp(2j * np.pi / PATCH * (k * a % PATCH))
                forward[cell, patch] = np.conj(wave)
                backward[patch, :, cell] = wave * window[a] / PATCH
    return forward.reshape(cells, -1), backward.reshape(-1, cells)


def filter_tables(gate_rows, looks):
    gate_starts = range(-HALF, gate_rows - HALF + 1, HALF)
    line_starts = range(0, looks + 1, HALF)
    gate_fwd, gate_back = patch_maps(gate_rows, gate_starts)
    line_fwd, _ = patch_maps(looks + PATCH, line_starts)
    _, line_back = patch_maps(looks, [start - HALF for start in line_starts])
    used = len(line_starts) * PATCH
    width = -(-used // LANES) * LANES
    line_fwd = np.pad(line_fwd, ((0, 0), (0, width - used)))
    line_back = np.pad(line_back, ((0, width - used), (0, 0)))
    block = right_block(line_fwd).reshape(2, looks + PATCH, 2 * width)
    enter = np.zeros((2, 4 * looks, 2 * width))
    for parity in range(2):
        for part in range(2):
            enter[parity, part * looks : (part + 1) * looks] = block[part, HALF : HALF + looks]
            low = 2 * looks + parity * 4 * HALF + part * 2 * HALF
            enter[parity, low : low + HALF] = block[part, :HALF]
            enter[parity, low + HALF : low + 2 * HALF] = block[part, HALF + looks :]
    enter = np.stack([split_table(table) for table in enter])
    gap = (np.arange(PATCH)[:, None] - np.arange(PATCH)[None, :]) % PATCH
    near = (gap <= 1) | (gap == PATCH - 1)
    bf16 = ml_dtypes.bfloat16
    near_gate = np.kron(np.eye(len(gate_starts)), near).astype(bf16)
    near_line = np.kron(np.eye(width // PATCH), near).astype(bf16)
    level = np.kron(np.eye(width // PATCH), np.ones((PATCH, PATCH)) / PATCH**2).astype(bf16)
    return (
        enter,
        split_table(left_block(gate_fwd.T)),
        near_gate,
        near_line,
        level,
        split_table(left_block(gate_back.T)),
        split_table(right_block(line_back)),
    )


def filter_kernel(
    looks_ref, enter_ref, gate_ref, near_gate_ref, near_line_ref, level_ref, gate_back_ref, line_back_ref,
    out_ref,
):
    shards, slab_rows, lanes = looks_ref.shape
    dates, _, gate_rows, looks = out_ref.shape
    gate_looks = gate_rows // shards
    received = looks_ref[...].astype(jnp.float32)

    def slab(index):
        return received[:, index * gate_looks : (index + 1) * gate_looks].reshape(gate_rows, lanes)

    for date in range(dates):
        cells = jnp.concatenate([slab(date), slab(dates + date // 2)], axis=1).astype(jnp.bfloat16)
        half = mm(cells, enter_ref[date % 2, 0]) + mm(cells, enter_ref[date % 2, 1])
        width = half.shape[1] // 2
        both = jnp.concatenate([half[:, :width], half[:, width:]], axis=0)
        spectra = table_times(gate_ref, both)
        rows = spectra.shape[0] // 2
        re, im = spectra[:rows], spectra[rows:]
        power = re * re + im * im
        near = mm(near_gate_ref[...], power.astype(jnp.bfloat16))
        near = mm(near.astype(jnp.bfloat16), near_line_ref[...])
        sums = jnp.sum(power.reshape(rows // PATCH, PATCH, width), axis=1)
        level = exact_times(sums, level_ref[...])
        scale = 1.0 / (9.0 * (level + 1e-06))
        near = near.reshape(rows // PATCH, PATCH, width) * scale[:, None, :]
        weight = jnp.sqrt(near + BOX_FLOOR).reshape(rows, width)
        weighted = jnp.concatenate([re * weight, im * weight], axis=0)
        image = table_times(gate_back_ref, weighted)
        image = jnp.concatenate([image[:gate_rows], image[gate_rows:]], axis=1)
        result = times_table(image, line_back_ref)
        out_ref[date, 0] = result[:, :looks]
        out_ref[date, 1] = result[:, looks:]


def filter_looks(received, dates, gate_rows, looks):
    tables = filter_tables(gate_rows, looks)
    return pl.pallas_call(
        filter_kernel,
        in_specs=[VMEM] * (1 + len(tables)),
        out_specs=VMEM,
        out_shape=jax.ShapeDtypeStruct((dates, 2, gate_rows, looks), jnp.float32),
        name="goldstein",
    )(received, *tables)


def exchange(blocks):
    return lax.all_to_all(blocks, "lines", split_axis=0, concat_axis=0, tiled=True)


def body(raw_echo, range_filter, azimuth_phase, pair_offset):
    shards = lax.axis_size("lines")
    dates, _, line_count, gates = raw_echo.shape
    gate_cols, line_total = azimuth_phase.shape
    columns = exchange(compress(raw_echo, range_filter, shards))
    phase = azimuth_phase.reshape(gate_cols, line_count, shards).transpose(2, 0, 1)
    looks = focus_looks(columns, jnp.cos(phase), jnp.sin(phase), pair_offset)
    return filter_looks(exchange(looks), dates, gates // ML_RG, line_count // ML_AZ)


def solution(mesh):
    placed = (P("groups", None, "lines", None), P(), P("lines", None), P())
    return jax.shard_map(
        body,
        mesh=mesh,
        in_specs=placed,
        out_specs=P("groups", None, None, "lines"),
        check_vma=False,
    )
```

profile of v0, /device:TPU:0, one launch (start us, length us, event | category | flops | bytes accessed | tf_op | source)
XLA Modules:
  0.0 76.4 jit_solution(11615241585208890901)
XLA Ops:
  0.0 5.2 %compress.1 = bf16[16,4,2,32,128]{4,3,2,1,0:T(8,128)(2,1)} custom-call(bf16[4,2,128,512]{3,2,1,0:T(8,128)(2,1)} %raw_ref.1, bf16[2,512,512]{2,1,0:T(8,128)(2,1)} %filt_ref.1), custom_call_target="tpu_custom_call" | custom-call | tf_op jit(solution)/shard_map/compress/pallas_call | solution.py:107
  5.2 0.0 copy-start.1
  5.2 7.5 %all-to-all-start = ((bf16[16,4,2,32,128]{4,3,2,1,0:T(8,128)(2,1)}), bf16[16,4,2,32,128]{4,3,2,1,0:T(8,128)(2,1)S(1)}, u32[]{:S(2)}, u32[]{:S(2)}) async-start(bf16[16,4,2,32,128]{4,3,2,1,0:T(8,128)(2,1)} %compress.1), calls=%async_computation | async-start | bytes 2097152 | tf_op jit(solution)/shard_map/all_to_all | solution.py:342
  12.8 0.0 copy-done.1
  12.8 1.0 %fusion = (f32[32,2048]{1,0:T(8,128)S(1)}, f32[32,2048]{1,0:T(8,128)S(1)}) fusion(f32[32,2048]{1,0:T(8,128)S(1)} %copy-done.1), kind=kLoop, calls=%fused_computation | loop fusion | bytes 786432 | tf_op jit(solution)/shard_map/sin | solution.py:351
  13.8 0.3 copy.19
  14.1 1.1 %copy.20 = f32[32,128,16]{1,0,2:T(8,128)} copy(f32[32,128,16]{0,2,1:T(8,128)S(1)} %bitcast.4) | data formatting | bytes 524288 | tf_op jit(solution)/shard_map/cos | solution.py:351
  15.2 0.3 copy.21
  15.6 1.1 %copy.22 = f32[32,128,16]{1,0,2:T(8,128)} copy(f32[32,128,16]{0,2,1:T(8,128)S(1)} %bitcast.5) | data formatting | bytes 524288 | tf_op jit(solution)/shard_map/sin | solution.py:351
  16.7 19.0 %all-to-all-done.col_ref = bf16[16,4,2,32,128]{4,3,2,1,0:T(8,128)(2,1)S(1)} async-done(((bf16[16,4,2,32,128]{4,3,2,1,0:T(8,128)(2,1)}), bf16[16,4,2,32,128]{4,3,2,1,0:T(8,128)(2,1)S(1)}, u32[]{:S(2)}, u32[]{:S(2)}) %all-to-all-start) | async-done | bytes 1048608 | tf_op jit(solution)/shard_map/all_to_all | solution.py:342
  35.7 0.0 copy-start
  35.7 1.0 %copy-done = bf16[16,4,2,32,128]{4,3,2,1,0:T(8,128)(2,1)} copy-done((bf16[16,4,2,32,128]{4,3,2,1,0:T(8,128)(2,1)}, bf16[16,4,2,32,128]{4,3,2,1,0:T(8,128)(2,1)S(1)}, u32[]{:S(2)}) %copy-start) | copy-done | bytes 1048600
  36.6 10.2 %focus.1 = bf16[16,48,128]{2,1,0:T(8,128)(2,1)} custom-call(s32[4]{0:T(128)} %offset_ref.1, bf16[16,4,2,32,128]{4,3,2,1,0:T(8,128)(2,1)} %copy-done, f32[16,32,128]{2,1,0:T(8,128)} %bitcast.6, f32[16,32,128]{2,1,0:T(8,128)} %bitcast.7, f32[2,16,128]{2,1,0:T(8,128)} %constant.26.clone.twid_ref, bf16[2,256,256]{2,1,0:T(8,128)(2,1)} %constant.27.clone.fwd_ref, ...), custom_call_target="tpu_custom_call" | custom-call | tf_op jit(solution)/shard_map/focus/pallas_call | solution.py:217
  46.8 15.9 %all_to_all.10.looks_ref = bf16[16,48,128]{2,1,0:T(8,128)(2,1)} all-to-all(bf16[16,48,128]{2,1,0:T(8,128)(2,1)} %focus.1), channel_id=1, replica_groups=mesh['groups'=2,'lines'=16] {'lines'}, dimensions={0} | all-to-all | bytes 393216 | tf_op jit(solution)/shard_map/all_to_all | solution.py:342
  62.7 11.8 %goldstein.1 = f32[4,2,128,64]{3,2,1,0:T(8,128)} custom-call(bf16[16,48,128]{2,1,0:T(8,128)(2,1)} %all_to_all.10.looks_ref, bf16[2,2,256,512]{3,2,1,0:T(8,128)(2,1)} %constant.32.clone.enter_ref, bf16[2,576,256]{2,1,0:T(8,128)(2,1)} %constant.33.clone.gate_ref, bf16[288,288]{1,0:T(8,128)(2,1)} %constant.34.clone.near_gate_ref, ...), custom_call_target="tpu_custom_call" | custom-call | tf_op jit(solution)/shard_map/goldstein/pallas_call | solution.py:332
  74.5 1.9 %copy.23 = f32[4,2,128,64]{2,3,1,0:T(8,128)} copy(f32[4,2,128,64]{3,2,1,0:T(8,128)} %goldstein.1) | data formatting | bytes 524288 | tf_op jit(solution)/shard_map/goldstein/pallas_call | solution.py:332
Async XLA Ops:
  5.2 7.6 %copy-start.1 = (f32[32,2048]{1,0:T(8,128)S(1)}, f32[32,2048]{1,0:T(8,128)}, u32[]{:S(2)}) copy-start(f32[32,2048]{1,0:T(8,128)} %param.19) | copy-start | bytes 786436
  5.2 30.4 %all-to-all-start = ((bf16[16,4,2,32,128]{4,3,2,1,0:T(8,128)(2,1)}), bf16[16,4,2,32,128]{4,3,2,1,0:T(8,128)(2,1)S(1)}, u32[]{:S(2)}, u32[]{:S(2)}) async-start(bf16[16,4,2,32,128]{4,3,2,1,0:T(8,128)(2,1)} %compress.1), calls=%async_computation | async-start | bytes 2097152 | tf_op jit(solution)/shard_map/all_to_all | solution.py:342
  35.7 1.0 %copy-start = (bf16[16,4,2,32,128]{4,3,2,1,0:T(8,128)(2,1)}, bf16[16,4,2,32,128]{4,3,2,1,0:T(8,128)(2,1)S(1)}, u32[]{:S(2)}) copy-start(bf16[16,4,2,32,128]{4,3,2,1,0:T(8,128)(2,1)S(1)} %all-to-all-done.col_ref) | copy-start | bytes 3145732
where the time goes:
time: 76.8 us; the launch traced here: 76.4 us
  Pallas kernels  27.2 us (35%)
  waiting for transfers between devices  19 us (25%)
  blocking collectives  15.9 us (21%)
  starting transfers between devices  7.55 us (10%)
  local copies, waits for them, and re-layouts  6.77 us (9%)
    all_to_all x1, waiting for transfers between devices, exchange(): lax.all_to_all(blocks, 'lines', split_axis=0, concat_axis=0, tiled=True)  19 us
    all_to_all x1, blocking collectives, exchange(): lax.all_to_all(blocks, 'lines', split_axis=0, concat_axis=0, tiled=True)  15.9 us
    pallas_call x1, Pallas kernels, filter_looks(): pl.pallas_call(filter_kernel, in_specs=[VMEM] * (1 + len(tables)), out_sp...  11.8 us
    pallas_call x1, Pallas kernels, focus_looks(): pl.pallas_call(focus_kernel, grid_spec=pltpu.PrefetchScalarGridSpec(num_s...  10.2 us
    all_to_all x1, starting transfers between devices, exchange(): lax.all_to_all(blocks, 'lines', split_axis=0, concat_axis=0, tiled=True)  7.55 us
    pallas_call x1, Pallas kernels, compress(): pl.pallas_call(compress_kernel, grid=(dates,), in_specs=[pl.BlockSpec((1,...  5.24 us
    sin x3, local copies, waits for them, and re-layouts, body(): looks = focus_looks(columns, jnp.cos(phase), jnp.sin(phase), pair_offset)  2.41 us
    pallas_call x1, local copies, waits for them, and re-layouts, filter_looks(): pl.pallas_call(filter_kernel, in_specs=[VMEM] * (1 + len(tables)), out_sp...  1.93 us
  transfers between devices with their start and end apart: 1, of which 1 were waited for; matrix products, arithmetic and copies ran while one was open for 5% of the time, Pallas kernels for 0%

commit v1 on v0

v1 whole, which is shorter than its diff:
```python
import functools

import jax
import jax.numpy as jnp
import ml_dtypes
import numpy as np
from jax import lax
from jax.experimental import pallas as pl
from jax.experimental.pallas import tpu as pltpu
from jax.sharding import PartitionSpec as P

ML_RG = 4
ML_AZ = 2
PATCH = 32
HALF = PATCH // 2
BOX_FLOOR = 0.25
LANES = 128
VMEM = pl.BlockSpec(memory_space=pltpu.VMEM)


def split_table(table):
    high = table.astype(np.float32).astype(ml_dtypes.bfloat16)
    low = (table - high.astype(np.float64)).astype(np.float32).astype(ml_dtypes.bfloat16)
    return np.stack([high, low])


def right_block(table):
    return np.block([[table.real, table.imag], [-table.imag, table.real]])


def left_block(table):
    return np.block([[table.real, -table.imag], [table.imag, table.real]])


def split(value):
    high = value.astype(jnp.bfloat16)
    low = (value - high.astype(jnp.float32)).astype(jnp.bfloat16)
    return high, low


def mm(a, b):
    return jnp.dot(a, b, preferred_element_type=jnp.float32)


def times_table(value, table):
    high, low = split(value)
    return mm(high, table[0]) + mm(low, table[0]) + mm(high, table[1])


def exact_times(value, table):
    high, low = split(value)
    return mm(high, table) + mm(low, table)


def times_exact(table, value):
    high, low = split(value)
    return mm(table, high) + mm(table, low)


def fft_leading(re, im, sign):
    count = len(re)
    if count == 1:
        return re, im
    if count == 2:
        return [re[0] + re[1], re[0] - re[1]], [im[0] + im[1], im[0] - im[1]]
    er, ei = fft_leading(re[0::2], im[0::2], sign)
    odr, odi = fft_leading(re[1::2], im[1::2], sign)
    half = count // 2
    out_r, out_i = [None] * count, [None] * count
    for k in range(half):
        angle = sign * 2.0 * np.pi * k / count
        c, s = float(np.cos(angle)), float(np.sin(angle))
        if k == 0:
            tr, ti = odr[k], odi[k]
        elif 4 * k == count:
            tr, ti = (-odi[k], odr[k]) if sign > 0 else (odi[k], -odr[k])
        else:
            tr = odr[k] * c - odi[k] * s
            ti = odr[k] * s + odi[k] * c
        out_r[k], out_i[k] = er[k] + tr, ei[k] + ti
        out_r[k + half], out_i[k + half] = er[k] - tr, ei[k] - ti
    return out_r, out_i


def stack_kernel(
    shards, offset_ref, raw_ref, filt_ref, phase_ref, twid_ref, fwd_ref, back_ref, gate_ref, main_ref, rim_ref,
    out_ref, sent, columns, trig, work, focused, looks_sent, looks_got, send_sem, recv_sem,
):
    dates, _, line_count, total_gates = raw_ref.shape
    gates, lanes = columns.shape[3], columns.shape[4]
    rows = shards * gates
    me = lax.axis_index("lines")

    def ring(step):
        return lax.rem(me + step, shards)

    barrier = pltpu.get_barrier_semaphore()

    @pl.loop(1, shards)
    def _(step):
        pl.semaphore_signal(barrier, inc=1, device_id={"lines": ring(step)}, device_id_type=pl.DeviceIdType.MESH)

    def compress(date):
        weights = filt_ref[...].reshape(2 * total_gates, total_gates)
        contract = (((1,), (1,)), ((), ()))
        first = lax.dot_general(weights, raw_ref[date, 0], contract, preferred_element_type=jnp.float32)
        second = lax.dot_general(weights, raw_ref[date, 1], contract, preferred_element_type=jnp.float32)
        real = first[:total_gates] - second[total_gates:]
        imag = first[total_gates:] + second[:total_gates]
        shape = (shards, gates, line_count)
        sent[date, :, 0] = real.astype(jnp.bfloat16).reshape(shape)
        sent[date, :, 1] = imag.astype(jnp.bfloat16).reshape(shape)

    def block(source, target, slot, peer):
        return pltpu.make_async_remote_copy(
            src_ref=source, dst_ref=target, send_sem=send_sem.at[slot], recv_sem=recv_sem.at[slot],
            device_id={"lines": peer}, device_id_type=pl.DeviceIdType.MESH,
        )

    def send_date(date):
        @pl.loop(1, shards)
        def _(step):
            peer = ring(step)
            block(sent.at[date, peer], columns.at[date, me], date, peer).start()

        columns[date, me] = sent[date, me]

    def arrived(date):
        part = pl.ds(0, shards - 1)
        return block(sent.at[date, part], columns.at[date, part], date, ring(1))

    compress(0)
    pl.semaphore_wait(barrier, shards - 1)
    send_date(0)

    @pl.loop(1, dates)
    def _(date):
        compress(date)
        send_date(date)

    trig[0] = jnp.cos(phase_ref[...].reshape(rows, lanes))
    trig[1] = jnp.sin(phase_ref[...].reshape(rows, lanes))
    chunk = min(gates, 8)

    @pl.loop(0, dates)
    def _(date):
        arrived(date).wait_recv()
        for start in range(0, gates, chunk):
            part = pl.ds(start, chunk)
            re = [columns[date, s, 0, part, :].astype(jnp.float32) for s in range(shards)]
            im = [columns[date, s, 1, part, :].astype(jnp.float32) for s in range(shards)]
            re, im = fft_leading(re, im, -1.0)
            for k in range(shards):
                c, s = twid_ref[0, pl.ds(k, 1), :], twid_ref[1, pl.ds(k, 1), :]
                at = pl.ds(k * gates + start, chunk)
                work[at, :lanes] = re[k] * c + im[k] * s
                work[at, lanes:] = im[k] * c - re[k] * s
        spectrum = times_table(work[...], fwd_ref)
        c, s = trig[0], trig[1]
        re, im = spectrum[:, :lanes], spectrum[:, lanes:]
        shifted = jnp.concatenate([re * c - im * s, re * s + im * c], axis=1)
        work[...] = times_table(shifted, back_ref)
        for start in range(0, gates, chunk):
            re, im = [], []
            for k in range(shards):
                c, s = twid_ref[0, pl.ds(k, 1), :], twid_ref[1, pl.ds(k, 1), :]
                at = pl.ds(k * gates + start, chunk)
                a, b = work[at, :lanes], work[at, lanes:]
                re.append(a * c - b * s)
                im.append(b * c + a * s)
            re, im = fft_leading(re, im, 1.0)
            for n in range(shards):
                at = pl.ds(n * gates + start, chunk)
                focused[date, at, :lanes] = re[n].astype(jnp.bfloat16).astype(jnp.float32)
                focused[date, at, lanes:] = im[n].astype(jnp.bfloat16).astype(jnp.float32)

    looks_rows = gate_ref.shape[0] // 3
    gate_looks = looks_rows // shards
    pieces, rims = [], []
    for d in range(dates):
        partner = lax.rem(d + offset_ref[d], dates)
        a, b = focused[d, :, :lanes], focused[d, :, lanes:]
        p, q = focused[partner, :, :lanes], focused[partner, :, lanes:]
        joined = jnp.concatenate([a * p + b * q, b * p - a * q], axis=1)
        summed = times_exact(gate_ref[...], joined)
        pieces.append(exact_times(summed[:looks_rows], main_ref[...]))
        sides = jnp.concatenate([summed[looks_rows : 2 * looks_rows], summed[2 * looks_rows :]], axis=1)
        side = exact_times(sides, rim_ref[d % 2])
        if d % 2 == 0:
            rims.append(side)
        else:
            rims[-1] = rims[-1] + side
    shaped = [piece.reshape(shards, gate_looks, lanes) for piece in pieces + rims]
    looks_sent[...] = jnp.concatenate(shaped, axis=1).astype(looks_sent.dtype)

    @pl.loop(1, shards)
    def _(step):
        peer = ring(step)
        block(looks_sent.at[peer], looks_got.at[me], dates, peer).start()

    looks_got[me] = looks_sent[me]

    @pl.loop(0, dates)
    def _(date):
        arrived(date).wait_send()

    part = pl.ds(0, shards - 1)
    last = block(looks_sent.at[part], looks_got.at[part], dates, ring(1))
    last.wait_send()
    last.wait_recv()
    out_ref[...] = looks_got[...]


def focus_tables(shards, gates, lanes):
    total = shards * lanes
    k1, n2 = np.arange(shards), np.arange(lanes)
    angle = 2.0 * np.pi / total * (np.outer(k1, n2) % total)
    twiddle = np.stack([np.cos(angle), np.sin(angle)]).astype(np.float32)
    grid = np.exp(-2j * np.pi / lanes * (np.outer(n2, n2) % lanes))
    forward = split_table(right_block(grid))
    backward = split_table(right_block(np.conj(grid)) / total)
    group = np.kron(np.eye(gates // ML_RG), np.ones((1, ML_RG)))
    before = np.eye(shards, k=-1)
    after = np.eye(shards, k=1)
    gate_sum = np.concatenate([np.kron(m, group) for m in (np.eye(shards), before, after)])
    looks = lanes // ML_AZ
    pair = np.kron(np.eye(looks), np.ones((ML_AZ, 1))) / (ML_RG * ML_AZ)
    main = np.kron(np.eye(2), pair)
    rim = np.zeros((2, 4 * lanes, lanes))
    for parity in range(2):
        for part in range(2):
            low = parity * 4 * HALF + part * 2 * HALF
            source = part * lanes
            rim[parity, source : source + lanes, low : low + HALF] = pair[:, looks - HALF :]
            source += 2 * lanes
            rim[parity, source : source + lanes, low + HALF : low + 2 * HALF] = pair[:, :HALF]
    bf16 = ml_dtypes.bfloat16
    return twiddle, forward, backward, gate_sum.astype(bf16), main.astype(bf16), rim.astype(bf16)


def exchanged_looks(raw_echo, range_filter, phase, pair_offset):
    dates, _, line_count, _ = raw_echo.shape
    shards, gates, lanes = phase.shape
    tables = focus_tables(shards, gates, lanes)
    rows = shards * gates
    slab_rows = (dates + dates // 2) * (gates // ML_RG)
    block = (shards, slab_rows, lanes)
    columns = (dates, shards, 2, gates, line_count)
    return pl.pallas_call(
        functools.partial(stack_kernel, shards),
        in_specs=[pl.BlockSpec(memory_space=pltpu.SMEM)] + [VMEM] * (3 + len(tables)),
        out_specs=VMEM,
        out_shape=jax.ShapeDtypeStruct(block, jnp.bfloat16),
        scratch_shapes=[
            pltpu.VMEM(columns, jnp.bfloat16),
            pltpu.VMEM(columns, jnp.bfloat16),
            pltpu.VMEM((2, rows, lanes), jnp.float32),
            pltpu.VMEM((rows, 2 * lanes), jnp.float32),
            pltpu.VMEM((dates, rows, 2 * lanes), jnp.float32),
            pltpu.VMEM(block, jnp.bfloat16),
            pltpu.VMEM(block, jnp.bfloat16),
            pltpu.SemaphoreType.DMA((dates + 1,)),
            pltpu.SemaphoreType.DMA((dates + 1,)),
        ],
        compiler_params=pltpu.CompilerParams(collective_id=0, has_side_effects=True),
        name="stack",
    )(pair_offset, raw_echo, range_filter, phase, *tables)


def tri_window():
    return 1.0 - np.abs(np.arange(PATCH) - (PATCH - 1) / 2.0) / HALF


def patch_maps(cells, starts):
    count = len(starts)
    forward = np.zeros((cells, count, PATCH), np.complex128)
    backward = np.zeros((count, PATCH, cells), np.complex128)
    window, k = tri_window(), np.arange(PATCH)
    for patch, start in enumerate(starts):
        for a in range(PATCH):
            cell = start + a
            if 0 <= cell < cells:
                wave = np.exp(2j * np.pi / PATCH * (k * a % PATCH))
                forward[cell, patch] = np.conj(wave)
                backward[patch, :, cell] = wave * window[a] / PATCH
    return forward.reshape(cells, -1), backward.reshape(-1, cells)


def filter_tables(gate_rows, looks):
    gate_starts = range(-HALF, gate_rows - HALF + 1, HALF)
    line_starts = range(0, looks + 1, HALF)
    gate_fwd, gate_back = patch_maps(gate_rows, gate_starts)
    line_fwd, _ = patch_maps(looks + PATCH, line_starts)
    _, line_back = patch_maps(looks, [start - HALF for start in line_starts])
    used = len(line_starts) * PATCH
    width = -(-used // LANES) * LANES
    line_fwd = np.pad(line_fwd, ((0, 0), (0, width - used)))
    line_back = np.pad(line_back, ((0, width - used), (0, 0)))
    block = right_block(line_fwd).reshape(2, looks + PATCH, 2 * width)
    enter = np.zeros((2, 4 * looks, 2 * width))
    for parity in range(2):
        for part in range(2):
            enter[parity, part * looks : (part + 1) * looks] = block[part, HALF : HALF + looks]
            low = 2 * looks + parity * 4 * HALF + part * 2 * HALF
            enter[parity, low : low + HALF] = block[part, :HALF]
            enter[parity, low + HALF : low + 2 * HALF] = block[part, HALF + looks :]
    gap = (np.arange(PATCH)[:, None] - np.arange(PATCH)[None, :]) % PATCH
    near = (gap <= 1) | (gap == PATCH - 1)
    bf16 = ml_dtypes.bfloat16
    near_gate = np.kron(np.eye(len(gate_starts)), near).astype(bf16)
    near_line = np.kron(np.eye(width // PATCH), near).astype(bf16)
    level = np.kron(np.eye(width // PATCH), np.ones((PATCH, PATCH)) / PATCH**2).astype(bf16)
    return (
        enter.astype(bf16),
        left_block(gate_fwd.T).astype(bf16),
        near_gate,
        near_line,
        level,
        left_block(gate_back.T).astype(bf16),
        right_block(line_back).T.astype(bf16),
    )


def filter_kernel(
    looks_ref, enter_ref, gate_ref, near_gate_ref, near_line_ref, level_ref, gate_back_ref, line_back_ref,
    out_ref,
):
    shards, slab_rows, lanes = looks_ref.shape
    dates, _, looks, gate_rows = out_ref.shape
    gate_looks = gate_rows // shards
    received = looks_ref[...].astype(jnp.float32)

    def slab(index):
        return received[:, index * gate_looks : (index + 1) * gate_looks].reshape(gate_rows, lanes)

    for date in range(dates):
        cells = jnp.concatenate([slab(date), slab(dates + date // 2)], axis=1).astype(jnp.bfloat16)
        half = mm(cells, enter_ref[date % 2]).astype(jnp.bfloat16)
        width = half.shape[1] // 2
        both = jnp.concatenate([half[:, :width], half[:, width:]], axis=0)
        spectra = mm(gate_ref[...], both)
        rows = spectra.shape[0] // 2
        re, im = spectra[:rows], spectra[rows:]
        power = re * re + im * im
        near = mm(near_gate_ref[...], power.astype(jnp.bfloat16))
        near = mm(near.astype(jnp.bfloat16), near_line_ref[...])
        sums = jnp.sum(power.reshape(rows // PATCH, PATCH, width), axis=1)
        level = exact_times(sums, level_ref[...])
        scale = 1.0 / (9.0 * (level + 1e-06))
        near = near.reshape(rows // PATCH, PATCH, width) * scale[:, None, :]
        weight = jnp.sqrt(near + BOX_FLOOR).reshape(rows, width)
        weighted = jnp.concatenate([re * weight, im * weight], axis=0).astype(jnp.bfloat16)
        image = mm(gate_back_ref[...], weighted).astype(jnp.bfloat16)
        image = jnp.concatenate([image[:gate_rows], image[gate_rows:]], axis=1)
        contract = (((1,), (1,)), ((), ()))
        result = lax.dot_general(line_back_ref[...], image, contract, preferred_element_type=jnp.float32)
        out_ref[date, 0] = result[:looks]
        out_ref[date, 1] = result[looks:]


def filter_looks(received, dates, gate_rows, looks):
    tables = filter_tables(gate_rows, looks)
    return pl.pallas_call(
        filter_kernel,
        in_specs=[VMEM] * (1 + len(tables)),
        out_specs=VMEM,
        out_shape=jax.ShapeDtypeStruct((dates, 2, looks, gate_rows), jnp.float32),
        name="goldstein",
    )(received, *tables)


def body(raw_echo, range_filter, azimuth_phase, pair_offset):
    shards = lax.axis_size("lines")
    dates, _, line_count, gates = raw_echo.shape
    gate_cols, line_total = azimuth_phase.shape
    phase = azimuth_phase.reshape(gate_cols, line_count, shards).transpose(2, 0, 1)
    received = exchanged_looks(raw_echo, range_filter, phase, pair_offset)
    image = filter_looks(received, dates, gates // ML_RG, line_count // ML_AZ)
    return image.transpose(0, 1, 3, 2)


def solution(mesh):
    placed = (P("groups", None, "lines", None), P(), P("lines", None), P())
    return jax.shard_map(
        body,
        mesh=mesh,
        in_specs=placed,
        out_specs=P("groups", None, None, "lines"),
        check_vma=False,
    )
```

time: 76.8 us -> 51.5 us (0.67)
  Pallas kernels: 27.2 us -> 48.9 us
  waiting for transfers between devices: 19 us -> 0 us
  blocking collectives: 15.9 us -> 0 us
  starting transfers between devices: 7.55 us -> 0 us
  local copies, waits for them, and re-layouts: 6.77 us -> 2.4 us
    pallas_call x2 -> x1, Pallas kernels: 15.4 us -> 41.6 us  [exchanged_looks(): pl.pallas_call(functools.partial(stack_kernel, shards), in_specs=[pl.Bloc...]
    all_to_all x1 -> x0, waiting for transfers between devices: 19 us -> none  [exchange(): lax.all_to_all(blocks, 'lines', split_axis=0, concat_axis=0, tiled=True)]
    all_to_all x1 -> x0, blocking collectives: 15.9 us -> none  [exchange(): lax.all_to_all(blocks, 'lines', split_axis=0, concat_axis=0, tiled=True)]
    all_to_all x1 -> x0, starting transfers between devices: 7.55 us -> none  [exchange(): lax.all_to_all(blocks, 'lines', split_axis=0, concat_axis=0, tiled=True)]
    pallas_call x1, Pallas kernels: 11.8 us -> 7.39 us  [filter_looks(): pl.pallas_call(filter_kernel, in_specs=[VMEM] * (1 + len(tables)), out_sp...]
    sin x3 -> x0, local copies, waits for them, and re-layouts: 2.41 us -> none  [body(): looks = focus_looks(columns, jnp.cos(phase), jnp.sin(phase), pair_offset)]
    pallas_call x1 -> x0, local copies, waits for them, and re-layouts: 1.93 us -> none  [filter_looks(): pl.pallas_call(filter_kernel, in_specs=[VMEM] * (1 + len(tables)), out_sp...]
    cos x2 -> x0, local copies, waits for them, and re-layouts: 1.45 us -> none  [body(): looks = focus_looks(columns, jnp.cos(phase), jnp.sin(phase), pair_offset)]
  transfers between devices with their start and end apart: 1 -> 0, of which waited for: 1 -> 0; matrix products, arithmetic and copies ran while one was open for 5% -> 0% of each run, Pallas kernels for 0% -> 0%
where the time goes in v1:
time: 51.5 us; the launch traced here: 51.4 us
  Pallas kernels  48.9 us (95%)
  local copies, waits for them, and re-layouts  2.4 us (5%)
    pallas_call x1, Pallas kernels, exchanged_looks(): pl.pallas_call(functools.partial(stack_kernel, shards), in_specs=[pl.Bloc...  41.6 us
    pallas_call x1, Pallas kernels, filter_looks(): pl.pallas_call(filter_kernel, in_specs=[VMEM] * (1 + len(tables)), out_sp...  7.39 us
    unnamed x1, local copies, waits for them, and re-layouts  1.28 us
    reshape x1, local copies, waits for them, and re-layouts, body(): azimuth_phase.reshape(gate_cols, line_count, shards).transpose(2, 0, 1)  1.13 us

profile of v1, /device:TPU:0, one launch (start us, length us, event | category | flops | bytes accessed | tf_op | source)
XLA Modules:
  0.0 51.4 jit_solution(13779546057352217793)
XLA Ops:
  0.0 1.3 %copy.18 = f32[32,2048]{0,1:T(8,128)S(1)} copy(f32[32,2048]{1,0:T(8,128)} %param.19) | data formatting | bytes 524288 | tf_op args[2]
  1.3 1.1 %copy.19 = f32[32,128,16]{1,0,2:T(8,128)} copy(f32[32,128,16]{0,2,1:T(8,128)S(1)} %bitcast.3) | data formatting | bytes 524288 | tf_op jit(solution)/shard_map/reshape | solution.py:376
  2.4 41.6 %stack.1.looks_ref = bf16[16,48,128]{2,1,0:T(8,128)(2,1)} custom-call(s32[4]{0:T(128)} %offset_ref.1, bf16[4,2,128,512]{3,2,1,0:T(8,128)(2,1)} %raw_ref.1, bf16[2,512,512]{2,1,0:T(8,128)(2,1)} %filt_ref.1, f32[16,32,128]{2,1,0:T(8,128)} %bitcast.4, f32[2,16,128]{2,1,0:T(8,128)} %constant.26.clone.twid_ref, bf16[2,256,256]{2,1,0:T(8,128)(2,1)} %constant.27.clone.fwd_ref, ...), custom_call_target="tpu_custom_call" | custom-call | tf_op jit(solution)/shard_map/stack/pallas_call | solution.py:249
  44.0 7.4 %goldstein.1 = f32[4,2,64,128]{3,2,1,0:T(8,128)} custom-call(bf16[16,48,128]{2,1,0:T(8,128)(2,1)} %stack.1.looks_ref, bf16[2,256,512]{2,1,0:T(8,128)(2,1)} %constant.32.clone.enter_ref, bf16[576,256]{1,0:T(8,128)(2,1)} %constant.33.clone.gate_ref, bf16[288,288]{1,0:T(8,128)(2,1)} %constant.34.clone.near_gate_ref, ...), custom_call_target="tpu_custom_call" | custom-call | tf_op jit(solution)/shard_map/goldstein/pallas_call | solution.py:363

commit v2 on v1

--- a/solution.py
+++ b/solution.py
@@ -50,11 +50,6 @@
 def exact_times(value, table):
     high, low = split(value)
     return mm(high, table) + mm(low, table)
-
-
-def times_exact(table, value):
-    high, low = split(value)
-    return mm(table, high) + mm(table, low)
 
 
 def fft_leading(re, im, sign):
@@ -82,17 +77,53 @@
     return out_r, out_i
 
 
+def filter_date(
+    cells, parity, date, enter_ref, gate_ref, near_gate_ref, near_line_ref, level_ref, gate_back_ref, line_back_ref,
+    out_ref,
+):
+    _, _, looks, gate_rows = out_ref.shape
+    half = mm(cells, enter_ref[parity]).astype(jnp.bfloat16)
+    width = half.shape[1] // 2
+    both = jnp.concatenate([half[:, :width], half[:, width:]], axis=0)
+    spectra = mm(gate_ref[...], both)
+    rows = spectra.shape[0] // 2
+    re, im = spectra[:rows], spectra[rows:]
+    power = re * re + im * im
+    near = mm(near_gate_ref[...], power.astype(jnp.bfloat16))
+    near = mm(near.astype(jnp.bfloat16), near_line_ref[...])
+    sums = jnp.sum(power.reshape(rows // PATCH, PATCH, width), axis=1)
+    level = exact_times(sums, level_ref[...])
+    scale = 1.0 / (9.0 * (level + 1e-06))
+    near = near.reshape(rows // PATCH, PATCH, width) * scale[:, None, :]
+    weight = jnp.sqrt(near + BOX_FLOOR).reshape(rows, width)
+    weighted = jnp.concatenate([re * weight, im * weight], axis=0).astype(jnp.bfloat16)
+    image = mm(gate_back_ref[...], weighted).astype(jnp.bfloat16)
+    image = jnp.concatenate([image[:gate_rows], image[gate_rows:]], axis=1)
+    contract = (((1,), (1,)), ((), ()))
+    result = lax.dot_general(line_back_ref[...], image, contract, preferred_element_type=jnp.float32)
+    out_ref[date, 0] = result[:looks]
+    out_ref[date, 1] = result[looks:]
+
+
 def stack_kernel(
-    shards, offset_ref, raw_ref, filt_ref, phase_ref, twid_ref, fwd_ref, back_ref, gate_ref, main_ref, rim_ref,
-    out_ref, sent, columns, trig, work, focused, looks_sent, looks_got, send_sem, recv_sem,
+    shards, offset_ref, raw_ref, filt_ref, phase_ref, *refs,
 ):
+    count = (len(refs) - 12) // 2
+    stored, out_ref, tables = refs[:count], refs[count], refs[count + 1 : 2 * count + 1]
+    (sent, columns, turned, trig, work, focused, looks_sent, looks_got,
+     send_sem, recv_sem, table_sem) = refs[2 * count + 1 :]
+    twid_ref, fwd_ref, back_ref, gate_ref, main_ref, rim_ref = tables[:6]
+    loads = [pltpu.make_async_copy(stored[i], tables[i], table_sem.at[i]) for i in range(count)]
+    for load in loads:
+        load.start()
     dates, _, line_count, total_gates = raw_ref.shape
     gates, lanes = columns.shape[3], columns.shape[4]
     rows = shards * gates
     me = lax.axis_index("lines")
 
     def ring(step):
-        return lax.rem(me + step, shards)
+        away = lax.div(step, 2) * (1 - 2 * lax.rem(step, 2)) + shards // 2
+        return lax.rem(me + away, shards)
 
     barrier = pltpu.get_barrier_semaphore()
 
@@ -138,8 +169,17 @@
         compress(date)
         send_date(date)
 
-    trig[0] = jnp.cos(phase_ref[...].reshape(rows, lanes))
-    trig[1] = jnp.sin(phase_ref[...].reshape(rows, lanes))
+    turned[...] = phase_ref[...].T
+
+    @pl.loop(0, shards)
+    def _(k):
+        phase = turned[pl.ds(k, lanes, stride=shards), :].T
+        at = pl.ds(pl.multiple_of(k * gates, gates), gates)
+        trig[0, at, :] = jnp.cos(phase)
+        trig[1, at, :] = jnp.sin(phase)
+
+    for load in loads[:6]:
+        load.wait()
     chunk = min(gates, 8)
 
     @pl.loop(0, dates)
@@ -176,39 +216,53 @@
 
     looks_rows = gate_ref.shape[0] // 3
     gate_looks = looks_rows // shards
-    pieces, rims = [], []
-    for d in range(dates):
-        partner = lax.rem(d + offset_ref[d], dates)
-        a, b = focused[d, :, :lanes], focused[d, :, lanes:]
-        p, q = focused[partner, :, :lanes], focused[partner, :, lanes:]
-        joined = jnp.concatenate([a * p + b * q, b * p - a * q], axis=1)
-        summed = times_exact(gate_ref[...], joined)
-        pieces.append(exact_times(summed[:looks_rows], main_ref[...]))
-        sides = jnp.concatenate([summed[looks_rows : 2 * looks_rows], summed[2 * looks_rows :]], axis=1)
-        side = exact_times(sides, rim_ref[d % 2])
-        if d % 2 == 0:
-            rims.append(side)
-        else:
-            rims[-1] = rims[-1] + side
-    shaped = [piece.reshape(shards, gate_looks, lanes) for piece in pieces + rims]
-    looks_sent[...] = jnp.concatenate(shaped, axis=1).astype(looks_sent.dtype)
-
-    @pl.loop(1, shards)
-    def _(step):
-        peer = ring(step)
-        block(looks_sent.at[peer], looks_got.at[me], dates, peer).start()
-
-    looks_got[me] = looks_sent[me]
+
+    def gathered(pair):
+        part = pl.ds(0, shards - 1)
+        return block(looks_sent.at[pair, part], looks_got.at[pair, part], dates + pair, ring(1))
+
+    for pair in range(dates // 2):
+        pieces, rim = [], None
+        for d in (2 * pair, 2 * pair + 1):
+            partner = lax.rem(d + offset_ref[d], dates)
+            a, b = focused[d, :, :lanes], focused[d, :, lanes:]
+            p, q = focused[partner, :, :lanes], focused[partner, :, lanes:]
+            joined = jnp.concatenate([a * p + b * q, b * p - a * q], axis=1).astype(jnp.bfloat16)
+            summed = mm(gate_ref[...], joined).astype(jnp.bfloat16)
+            pieces.append(mm(summed[:looks_rows], main_ref[...]))
+            sides = jnp.concatenate([summed[looks_rows : 2 * looks_rows], summed[2 * looks_rows :]], axis=1)
+            side = mm(sides, rim_ref[d % 2])
+            rim = side if rim is None else rim + side
+        shaped = [piece.reshape(shards, gate_looks, lanes) for piece in pieces + [rim]]
+        looks_sent[pair] = jnp.concatenate(shaped, axis=1).astype(looks_sent.dtype)
+
+        @pl.loop(1, shards)
+        def _(step):
+            peer = ring(step)
+            block(looks_sent.at[pair, peer], looks_got.at[pair, me], dates + pair, peer).start()
+
+        looks_got[pair, me] = looks_sent[pair, me]
+
+    for load in loads[6:]:
+        load.wait()
 
     @pl.loop(0, dates)
     def _(date):
         arrived(date).wait_send()
 
-    part = pl.ds(0, shards - 1)
-    last = block(looks_sent.at[part], looks_got.at[part], dates, ring(1))
-    last.wait_send()
-    last.wait_recv()
-    out_ref[...] = looks_got[...]
+    for pair in range(dates // 2):
+        gathered(pair).wait_recv()
+        received = looks_got[pair].astype(jnp.float32)
+
+        def slab(index):
+            return received[:, index * gate_looks : (index + 1) * gate_looks].reshape(shards * gate_looks, lanes)
+
+        for parity in range(2):
+            cells = jnp.concatenate([slab(parity), slab(2)], axis=1).astype(jnp.bfloat16)
+            filter_date(cells, parity, 2 * pair + parity, *tables[6:], out_ref)
+
+    for pair in range(dates // 2):
+        gathered(pair).wait_send()
 
 
 def focus_tables(shards, gates, lanes):
@@ -238,33 +292,38 @@
     return twiddle, forward, backward, gate_sum.astype(bf16), main.astype(bf16), rim.astype(bf16)
 
 
-def exchanged_looks(raw_echo, range_filter, phase, pair_offset):
-    dates, _, line_count, _ = raw_echo.shape
-    shards, gates, lanes = phase.shape
-    tables = focus_tables(shards, gates, lanes)
+def filtered_looks(raw_echo, range_filter, azimuth_phase, pair_offset, shards):
+    dates, _, lanes, total_gates = raw_echo.shape
+    gates = azimuth_phase.shape[0]
+    tables = focus_tables(shards, gates, lanes) + filter_tables(total_gates // ML_RG, lanes // ML_AZ)
     rows = shards * gates
-    slab_rows = (dates + dates // 2) * (gates // ML_RG)
-    block = (shards, slab_rows, lanes)
-    columns = (dates, shards, 2, gates, line_count)
+    pairs = dates // 2
+    block = (pairs, shards, 3 * (gates // ML_RG), lanes)
+    columns = (dates, shards, 2, gates, lanes)
     return pl.pallas_call(
         functools.partial(stack_kernel, shards),
-        in_specs=[pl.BlockSpec(memory_space=pltpu.SMEM)] + [VMEM] * (3 + len(tables)),
+        in_specs=[pl.BlockSpec(memory_space=pltpu.SMEM)]
+        + [VMEM] * 3
+        + [pl.BlockSpec(memory_space=pl.ANY)] * len(tables),
         out_specs=VMEM,
-        out_shape=jax.ShapeDtypeStruct(block, jnp.bfloat16),
-        scratch_shapes=[
+        out_shape=jax.ShapeDtypeStruct((dates, 2, lanes // ML_AZ, total_gates // ML_RG), jnp.float32),
+        scratch_shapes=[pltpu.VMEM(table.shape, table.dtype) for table in tables]
+        + [
             pltpu.VMEM(columns, jnp.bfloat16),
             pltpu.VMEM(columns, jnp.bfloat16),
+            pltpu.VMEM(azimuth_phase.shape[::-1], jnp.float32),
             pltpu.VMEM((2, rows, lanes), jnp.float32),
             pltpu.VMEM((rows, 2 * lanes), jnp.float32),
             pltpu.VMEM((dates, rows, 2 * lanes), jnp.float32),
             pltpu.VMEM(block, jnp.bfloat16),
             pltpu.VMEM(block, jnp.bfloat16),
-            pltpu.SemaphoreType.DMA((dates + 1,)),
-            pltpu.SemaphoreType.DMA((dates + 1,)),
+            pltpu.SemaphoreType.DMA((dates + pairs,)),
+            pltpu.SemaphoreType.DMA((dates + pairs,)),
+            pltpu.SemaphoreType.DMA((len(tables),)),
         ],
         compiler_params=pltpu.CompilerParams(collective_id=0, has_side_effects=True),
         name="stack",
-    )(pair_offset, raw_echo, range_filter, phase, *tables)
+    )(pair_offset, raw_echo, range_filter, azimuth_phase, *tables)
 
 
 def tri_window():
@@ -321,61 +380,9 @@
     )
 
 
-def filter_kernel(
-    looks_ref, enter_ref, gate_ref, near_gate_ref, near_line_ref, level_ref, gate_back_ref, line_back_ref,
-    out_ref,
-):
-    shards, slab_rows, lanes = looks_ref.shape
-    dates, _, looks, gate_rows = out_ref.shape
-    gate_looks = gate_rows // shards
-    received = looks_ref[...].astype(jnp.float32)
-
-    def slab(index):
-        return received[:, index * gate_looks : (index + 1) * gate_looks].reshape(gate_rows, lanes)
-
-    for date in range(dates):
-        cells = jnp.concatenate([slab(date), slab(dates + date // 2)], axis=1).astype(jnp.bfloat16)
-        half = mm(cells, enter_ref[date % 2]).astype(jnp.bfloat16)
-        width = half.shape[1] // 2
-        both = jnp.concatenate([half[:, :width], half[:, width:]], axis=0)
-        spectra = mm(gate_ref[...], both)
-        rows = spectra.shape[0] // 2
-        re, im = spectra[:rows], spectra[rows:]
-        power = re * re + im * im
-        near = mm(near_gate_ref[...], power.astype(jnp.bfloat16))
-        near = mm(near.astype(jnp.bfloat16), near_line_ref[...])
-        sums = jnp.sum(power.reshape(rows // PATCH, PATCH, width), axis=1)
-        level = exact_times(sums, level_ref[...])
-        scale = 1.0 / (9.0 * (level + 1e-06))
-        near = near.reshape(rows // PATCH, PATCH, width) * scale[:, None, :]
-        weight = jnp.sqrt(near + BOX_FLOOR).reshape(rows, width)
-        weighted = jnp.concatenate([re * weight, im * weight], axis=0).astype(jnp.bfloat16)
-        image = mm(gate_back_ref[...], weighted).astype(jnp.bfloat16)
-        image = jnp.concatenate([image[:gate_rows], image[gate_rows:]], axis=1)
-        contract = (((1,), (1,)), ((), ()))
-        result = lax.dot_general(line_back_ref[...], image, contract, preferred_element_type=jnp.float32)
-        out_ref[date, 0] = result[:looks]
-        out_ref[date, 1] = result[looks:]
-
-
-def filter_looks(received, dates, gate_rows, looks):
-    tables = filter_tables(gate_rows, looks)
-    return pl.pallas_call(
-        filter_kernel,
-        in_specs=[VMEM] * (1 + len(tables)),
-        out_specs=VMEM,
-        out_shape=jax.ShapeDtypeStruct((dates, 2, looks, gate_rows), jnp.float32),
-        name="goldstein",
-    )(received, *tables)
-
-
 def body(raw_echo, range_filter, azimuth_phase, pair_offset):
     shards = lax.axis_size("lines")
-    dates, _, line_count, gates = raw_echo.shape
-    gate_cols, line_total = azimuth_phase.shape
-    phase = azimuth_phase.reshape(gate_cols, line_count, shards).transpose(2, 0, 1)
-    received = exchanged_looks(raw_echo, range_filter, phase, pair_offset)
-    image = filter_looks(received, dates, gates // ML_RG, line_count // ML_AZ)
+    image = filtered_looks(raw_echo, range_filter, azimuth_phase, pair_offset, shards)
     return image.transpose(0, 1, 3, 2)
 
 

time: 51.5 us -> 47.4 us (0.920)
  Pallas kernels: 48.9 us -> 45.6 us
  local copies, waits for them, and re-layouts: 2.4 us -> 1.67 us
    pallas_call x2 -> x1, Pallas kernels: 48.9 us -> 45.6 us  [filtered_looks(): pl.pallas_call(functools.partial(stack_kernel, shards), in_specs=[pl.Bloc...]
    reshape x1 -> x0, local copies, waits for them, and re-layouts: 1.13 us -> none  [body(): azimuth_phase.reshape(gate_cols, line_count, shards).transpose(2, 0, 1)]
where the time goes in v2:
time: 47.4 us; the launch traced here: 47.3 us
  Pallas kernels  45.6 us (96%)
  local copies, waits for them, and re-layouts  1.67 us (4%)
    pallas_call x1, Pallas kernels, filtered_looks(): pl.pallas_call(functools.partial(stack_kernel, shards), in_specs=[pl.Bloc...  45.6 us
    unnamed x1, local copies, waits for them, and re-layouts  1.67 us

profile of v2, /device:TPU:0, one launch (start us, length us, event | category | flops | bytes accessed | tf_op | source)
XLA Modules:
  0.0 47.3 jit_solution(6927596507532779759)
XLA Ops:
  0.0 45.6 %stack.1 = f32[4,2,64,128]{3,2,1,0:T(8,128)} custom-call(s32[4]{0:T(128)} %offset_ref.1, bf16[4,2,128,512]{3,2,1,0:T(8,128)(2,1)} %raw_ref.1, bf16[2,512,512]{2,1,0:T(8,128)(2,1)} %filt_ref.1, f32[32,2048]{1,0:T(8,128)} %phase_ref.1, f32[2,16,128]{2,1,0:T(8,128)} %constant.26.clone.refs_0_, bf16[2,256,256]{2,1,0:T(8,128)(2,1)} %constant.27.clone.refs_1_, ...), custom_call_target="tpu_custom_call" | custom-call | tf_op jit(solution)/shard_map/stack/pallas_call | solution.py:303
  45.6 1.7 %copy.19 = f32[4,2,128,64]{2,3,1,0:T(8,128)} copy(f32[4,2,128,64]{2,3,1,0:T(8,128)} %bitcast.1) | data formatting | bytes 524288

commit v3 on v2

--- a/solution.py
+++ b/solution.py
@@ -18,12 +18,6 @@
 VMEM = pl.BlockSpec(memory_space=pltpu.VMEM)
 
 
-def split_table(table):
-    high = table.astype(np.float32).astype(ml_dtypes.bfloat16)
-    low = (table - high.astype(np.float64)).astype(np.float32).astype(ml_dtypes.bfloat16)
-    return np.stack([high, low])
-
-
 def right_block(table):
     return np.block([[table.real, table.imag], [-table.imag, table.real]])
 
@@ -40,11 +34,6 @@
 
 def mm(a, b):
     return jnp.dot(a, b, preferred_element_type=jnp.float32)
-
-
-def times_table(value, table):
-    high, low = split(value)
-    return mm(high, table[0]) + mm(low, table[0]) + mm(high, table[1])
 
 
 def exact_times(value, table):
@@ -122,8 +111,7 @@
     me = lax.axis_index("lines")
 
     def ring(step):
-        away = lax.div(step, 2) * (1 - 2 * lax.rem(step, 2)) + shards // 2
-        return lax.rem(me + away, shards)
+        return lax.rem(me + step, shards)
 
     barrier = pltpu.get_barrier_semaphore()
 
@@ -195,11 +183,11 @@
                 at = pl.ds(k * gates + start, chunk)
                 work[at, :lanes] = re[k] * c + im[k] * s
                 work[at, lanes:] = im[k] * c - re[k] * s
-        spectrum = times_table(work[...], fwd_ref)
+        spectrum = mm(work[...].astype(jnp.bfloat16), fwd_ref[...])
         c, s = trig[0], trig[1]
         re, im = spectrum[:, :lanes], spectrum[:, lanes:]
         shifted = jnp.concatenate([re * c - im * s, re * s + im * c], axis=1)
-        work[...] = times_table(shifted, back_ref)
+        work[...] = mm(shifted.astype(jnp.bfloat16), back_ref[...])
         for start in range(0, gates, chunk):
             re, im = [], []
             for k in range(shards):
@@ -271,8 +259,8 @@
     angle = 2.0 * np.pi / total * (np.outer(k1, n2) % total)
     twiddle = np.stack([np.cos(angle), np.sin(angle)]).astype(np.float32)
     grid = np.exp(-2j * np.pi / lanes * (np.outer(n2, n2) % lanes))
-    forward = split_table(right_block(grid))
-    backward = split_table(right_block(np.conj(grid)) / total)
+    forward = right_block(grid)
+    backward = right_block(np.conj(grid)) / total
     group = np.kron(np.eye(gates // ML_RG), np.ones((1, ML_RG)))
     before = np.eye(shards, k=-1)
     after = np.eye(shards, k=1)
@@ -289,7 +277,7 @@
             source += 2 * lanes
             rim[parity, source : source + lanes, low + HALF : low + 2 * HALF] = pair[:, :HALF]
     bf16 = ml_dtypes.bfloat16
-    return twiddle, forward, backward, gate_sum.astype(bf16), main.astype(bf16), rim.astype(bf16)
+    return twiddle, forward.astype(bf16), backward.astype(bf16), gate_sum.astype(bf16), main.astype(bf16), rim.astype(bf16)
 
 
 def filtered_looks(raw_echo, range_filter, azimuth_phase, pair_offset, shards):

time: 47.4 us -> 46.1 us (0.973)
  Pallas kernels: 45.6 us -> 44.2 us
    pallas_call x1, Pallas kernels: 45.6 us -> 44.2 us  [filtered_looks(): pl.pallas_call(functools.partial(stack_kernel, shards), in_specs=[pl.Bloc...]
where the time goes in v3:
time: 46.1 us; the launch traced here: 45.9 us
  Pallas kernels  44.2 us (96%)
  local copies, waits for them, and re-layouts  1.67 us (4%)
    pallas_call x1, Pallas kernels, filtered_looks(): pl.pallas_call(functools.partial(stack_kernel, shards), in_specs=[pl.Bloc...  44.2 us
    unnamed x1, local copies, waits for them, and re-layouts  1.67 us

profile of v3, /device:TPU:0, one launch (start us, length us, event | category | flops | bytes accessed | tf_op | source)
XLA Modules:
  0.0 45.9 jit_solution(7940889892115631616)
XLA Ops:
  0.0 44.2 %stack.1 = f32[4,2,64,128]{3,2,1,0:T(8,128)} custom-call(s32[4]{0:T(128)} %offset_ref.1, bf16[4,2,128,512]{3,2,1,0:T(8,128)(2,1)} %raw_ref.1, bf16[2,512,512]{2,1,0:T(8,128)(2,1)} %filt_ref.1, f32[32,2048]{1,0:T(8,128)} %phase_ref.1, f32[2,16,128]{2,1,0:T(8,128)} %constant.26.clone.refs_0_, bf16[256,256]{1,0:T(8,128)(2,1)} %constant.27.clone.refs_1_, ...), custom_call_target="tpu_custom_call" | custom-call | tf_op jit(solution)/shard_map/stack/pallas_call | solution.py:291
  44.2 1.7 %copy.19 = f32[4,2,128,64]{2,3,1,0:T(8,128)} copy(f32[4,2,128,64]{2,3,1,0:T(8,128)} %bitcast.1) | data formatting | bytes 524288
